TPU v7x, 32 devices: a whole 2x2x4 slice. The times are simulated.
32 devices in a mesh: seq: 8 (over z, x), hid: 4 (over y, core).
Axes of the slice: x: 2, y: 2, z: 4, core: 2. Of those that a mesh axis runs over, the one named last changes fastest.
Arguments:
- tokens: bfloat16 [1024, 4096], P('seq', 'hid'), may hold values from -6 to 6
- hidden_grad: bfloat16 [1024, 14336], P('seq', 'hid'), may hold values from -6 to 6
- gate_blocks: bfloat16 [4, 448, 128, 128], P('hid', 'seq'), may hold values from -0.125 to 0.125
- up_blocks: bfloat16 [4, 448, 128, 128], P('hid', 'seq'), may hold values from -0.125 to 0.125
- gate_rows: int32 [4, 448], P('hid'), may hold values from 0 to 31, as said below
- gate_cols: int32 [4, 448], P('hid'), may hold values from 0 to 27
- gate_count: int32 [4], P('hid'), may hold values from 56 to 448, as said below
- up_rows: int32 [4, 448], P('hid'), may hold values from 0 to 31, as said below
- up_cols: int32 [4, 448], P('hid'), may hold values from 0 to 27
- up_count: int32 [4], P('hid'), may hold values from 56 to 448, as said below
Outputs:
- hidden: bfloat16 [1024, 14336], P('seq', 'hid')
- input_grad: bfloat16 [1024, 4096], P('seq', 'hid')
- gate_block_grads: bfloat16 [4, 448, 128, 128], P('hid', 'seq')
- up_block_grads: bfloat16 [4, 448, 128, 128], P('hid', 'seq')
Inputs may be any that keep to these rules, and one draw needn't show every extreme that they name: For each panel, the pairs (gate_rows, gate_cols) over all 448 slots are distinct. `gate_count`: slots at or after a panel's count hold no block of the matrix. For each panel, the pairs (up_rows, up_cols) over all 448 slots are distinct. `up_count`: slots at or after a panel's count hold no block of the matrix.
All inputs are finite; a program needn't handle non-finite values.
Results may differ from a plain program's by a relative error of at most 0.018.
Values may be sent and summed in bfloat16 or wider, within the bound.
A program may use at most 192 MiB of HBM per device.

v0:
```python
import math
import jax
import jax.numpy as jnp
from jax import lax
from jax.sharding import PartitionSpec as P


def swapped(value, axis, stride):
    mask = 2**stride
    pairs = [(source, source ^ mask) for source in range(lax.axis_size(axis))]
    return lax.ppermute(value, axis, pairs)


def silu_parts(preact):
    sigma = jax.nn.sigmoid(preact)
    return (preact * sigma, sigma * (1.0 + preact * (1.0 - sigma)))


def place_split(products, placing, form):
    high_part = products.astype(jnp.bfloat16)
    rest_part = (products - high_part.astype(jnp.float32)).astype(jnp.bfloat16)
    table = placing.astype(jnp.bfloat16)
    placed = jnp.einsum(form, high_part, table, preferred_element_type=jnp.float32)
    return placed + jnp.einsum(form, rest_part, table, preferred_element_type=jnp.float32)


def project_slots(tiles, weights, rows, columns, live_count, group_size, trips, col_blocks):
    tok_rows = tiles.shape[0]
    block_size = tiles.shape[2]
    targets = jnp.arange(col_blocks)
    offsets = jnp.arange(group_size)

    def project_one_group(group_index, running):
        start = group_index * group_size
        chosen = lax.dynamic_slice_in_dim(weights, start, group_size, 0)
        row_ids = lax.dynamic_slice_in_dim(rows, start, group_size, 0)
        col_ids = lax.dynamic_slice_in_dim(columns, start, group_size, 0)
        active = start + offsets < live_count
        picked = jnp.take(tiles, row_ids, axis=1)
        products = jnp.einsum("tsk,skn->tsn", picked, chosen, preferred_element_type=jnp.float32)
        placing = (col_ids[:, None] == targets[None, :]) & active[:, None]
        return running + place_split(products, placing, "tsn,sc->tcn")

    initial = jnp.zeros((tok_rows, col_blocks, block_size), jnp.float32)
    return lax.fori_loop(0, trips, project_one_group, initial)


def return_slots(grad_tiles, weights, rows, columns, live_count, group_size, trips, row_blocks):
    tok_rows = grad_tiles.shape[0]
    block_size = grad_tiles.shape[2]
    targets = jnp.arange(row_blocks)
    offsets = jnp.arange(group_size)

    def return_one_group(group_index, running):
        start = group_index * group_size
        chosen = lax.dynamic_slice_in_dim(weights, start, group_size, 0)
        row_ids = lax.dynamic_slice_in_dim(rows, start, group_size, 0)
        col_ids = lax.dynamic_slice_in_dim(columns, start, group_size, 0)
        active = start + offsets < live_count
        picked = jnp.take(grad_tiles, col_ids, axis=1)
        products = jnp.einsum("tsn,skn->tsk", picked, chosen, preferred_element_type=jnp.float32)
        placing = (row_ids[:, None] == targets[None, :]) & active[:, None]
        return running + place_split(products, placing, "tsk,sr->trk")

    initial = jnp.zeros((tok_rows, row_blocks, block_size), jnp.float32)
    return lax.fori_loop(0, trips, return_one_group, initial)


def on_device(
    tokens,
    hidden_grad,
    gate_blocks,
    up_blocks,
    gate_rows,
    gate_cols,
    gate_count,
    up_rows,
    up_cols,
    up_count,
):
    gathered = lax.all_gather(tokens, "hid", axis=1, tiled=True)
    tok_rows = gathered.shape[0]
    block_size = gate_blocks.shape[2]
    row_blocks = gathered.shape[1] // block_size
    col_blocks = hidden_grad.shape[1] // block_size
    gate_all = lax.all_gather(gate_blocks, "seq", axis=1, tiled=True)
    up_all = lax.all_gather(up_blocks, "seq", axis=1, tiled=True)
    capacity = gate_all.shape[1]
    group_size = 32
    groups = capacity // group_size
    gate_live = gate_count[0]
    up_live = up_count[0]
    tiles = gathered.reshape(tok_rows, row_blocks, block_size)
    gate_pre = project_slots(
        tiles, gate_all[0], gate_rows[0], gate_cols[0], gate_live, group_size, groups, col_blocks
    )
    up_pre = project_slots(
        tiles, up_all[0], up_rows[0], up_cols[0], up_live, group_size, groups, col_blocks
    )
    activated, slope = silu_parts(gate_pre)
    hidden = (activated * up_pre).astype(jnp.bfloat16)
    upstream = hidden_grad.reshape(tok_rows, col_blocks, block_size).astype(jnp.float32)
    gate_grad = (upstream * up_pre * slope).astype(jnp.bfloat16)
    up_grad = (upstream * activated).astype(jnp.bfloat16)
    input_sum = return_slots(
        gate_grad,
        gate_all[0],
        gate_rows[0],
        gate_cols[0],
        gate_live,
        group_size,
        groups,
        row_blocks,
    )
    input_sum = input_sum + return_slots(
        up_grad, up_all[0], up_rows[0], up_cols[0], up_live, group_size, groups, row_blocks
    )
    input_grad = lax.psum_scatter(
        input_sum.reshape(tok_rows, row_blocks * block_size).astype(jnp.bfloat16),
        "hid",
        scatter_dimension=1,
        tiled=True,
    )
    seq_count = lax.axis_size("seq")
    position = lax.axis_index("seq")
    levels = seq_count.bit_length() - 1
    blk_dev = capacity // seq_count
    other_tiles, other_gate, other_up = swapped((tiles, gate_grad, up_grad), "seq", 0)
    both_tiles = jnp.concatenate([tiles, other_tiles], axis=0)
    both_gate = jnp.concatenate([gate_grad, other_gate], axis=0)
    both_up = jnp.concatenate([up_grad, other_up], axis=0)
    parity = position % 2
    owners = 2 * jnp.arange(seq_count // 2) + parity
    slot_ids = (owners[:, None] * blk_dev + jnp.arange(blk_dev)[None, :]).reshape(-1)
    stacked = []
    for rows, columns, live_count, grad_tiles in (
        (gate_rows[0], gate_cols[0], gate_live, both_gate),
        (up_rows[0], up_cols[0], up_live, both_up),
    ):
        row_ids = jnp.take(rows, slot_ids)
        col_ids = jnp.take(columns, slot_ids)
        picked_input = jnp.take(both_tiles, row_ids, axis=1)
        picked_grad = jnp.take(grad_tiles, col_ids, axis=1)
        block_term = jnp.einsum(
            "tsk,tsn->skn", picked_input, picked_grad, preferred_element_type=jnp.float32
        )
        stacked.append(block_term * (slot_ids < live_count).astype(jnp.float32)[:, None, None])
    current = jnp.stack(stacked, axis=1)
    current = current.reshape((seq_count // 2, blk_dev) + current.shape[1:])
    for level in range(1, levels):
        own_bit = position // 2**level % 2
        halves = current.reshape((current.shape[0] // 2, 2) + current.shape[1:])
        kept = lax.dynamic_index_in_dim(halves, own_bit, 1, keepdims=False)
        sent = lax.dynamic_index_in_dim(halves, 1 - own_bit, 1, keepdims=False)
        received = swapped(sent.astype(jnp.bfloat16), "seq", level)
        current = kept + received.astype(jnp.float32)
    summed = current[0]
    scale = 1.0 / math.sqrt(tok_rows * seq_count)
    gate_block_grads = (summed[:, 0] * scale).astype(jnp.bfloat16)[None]
    up_block_grads = (summed[:, 1] * scale).astype(jnp.bfloat16)[None]
    return (
        hidden.reshape(tok_rows, col_blocks * block_size),
        input_grad,
        gate_block_grads,
        up_block_grads,
    )


def solution(mesh):
    placed = (
        P("seq", "hid"),
        P("seq", "hid"),
        P("hid", "seq", None, None),
        P("hid", "seq", None, None),
        P("hid", None),
        P("hid", None),
        P("hid"),
        P("hid", None),
        P("hid", None),
        P("hid"),
    )
    return jax.shard_map(
        on_device,
        mesh=mesh,
        in_specs=placed,
        out_specs=(
            P("seq", "hid"),
            P("seq", "hid"),
            P("hid", "seq", None, None),
            P("hid", "seq", None, None),
        ),
        check_vma=False,
    )
```

profile of v0, /device:TPU:0, one launch (start us, length us, event | category | flops | bytes accessed | tf_op | source)
XLA Modules:
  0.0 1165.3 jit_solution(1844786483724718215)
XLA Ops:
  16.3 13.3 %all-gather.6.cloned.1.call-done = bf16[128,4096]{0,1:T(8,128)(2,1)} async-done(((bf16[128,1024]{0,1:T(8,128)(2,1)}), bf16[128,4096]{0,1:T(8,128)(2,1)}) %all-gather.6.cloned.1.call-update) | async-done | bytes 1048592 | tf_op jit(solution)/shard_map/all_gather | solution.py:81
  33.3 200.2 %all-gather.8.cloned.1.call-done = bf16[1,448,128,128]{3,2,0,1:T(8,128)(2,1)} async-done(((bf16[1,56,128,128]{3,2,0,1:T(8,128)(2,1)}), bf16[1,448,128,128]{3,2,0,1:T(8,128)(2,1)}) %all-gather.8.cloned.1.call-update) | async-done | bytes 14680080 | tf_op jit(solution)/shard_map/all_gather | solution.py:87
  233.5 192.3 %while.61 = (s32[]{:T(128)}, f32[128,28,128]{2,1,0:T(8,128)}, s32[448]{0:T(512)S(1)}, s32[]{:T(128)}, bf16[448,128,128]{2,1,0:T(8,128)(2,1)}, /*index=5*/s32[448...) while((s32[]{:T(128)}, f32[128,28,128]{2,1,0:T(8,128)}, ...), condition=%wide.region_3.5_spmd.clone, body=%wide.region_2.4_spmd.clone.sunk | while | flops 196940544 | bytes 19928416 | solution.py:45
  256.7 3.7 bitcast_add_fusion.9
  284.1 3.7 bitcast_add_fusion.9
  311.5 4.6 bitcast_add_fusion.9
  326.1 3.7 bitcast_add_fusion.9
  353.5 3.7 bitcast_add_fusion.9
  394.6 3.9 bitcast_add_fusion.9
  425.8 9.8 all-gather.4.cloned.1.call-done
  435.6 193.2 %while.60 = (s32[]{:T(128)}, f32[128,28,128]{2,1,0:T(8,128)}, s32[448]{0:T(512)S(1)}, s32[]{:T(128)}, bf16[448,128,128]{2,1,0:T(8,128)(2,1)}, /*index=5*/s32[448...) while((s32[]{:T(128)}, f32[128,28,128]{2,1,0:T(8,128)}, ...), condition=%wide.region_1.3_spmd.clone, body=%wide.region_0.2_spmd.clone.sunk | while | flops 196940544 | bytes 19928416 | solution.py:45
  458.7 3.8 bitcast_add_fusion.8
  472.6 3.8 bitcast_add_fusion.8
  486.4 3.8 bitcast_add_fusion.8
  500.3 3.8 bitcast_add_fusion.8
  514.2 3.8 bitcast_add_fusion.8
  528.0 3.8 bitcast_add_fusion.8
  541.9 3.8 bitcast_add_fusion.8
  555.7 3.8 bitcast_add_fusion.8
  569.6 3.8 bitcast_add_fusion.8
  583.4 3.8 bitcast_add_fusion.8
  597.3 3.8 bitcast_add_fusion.8
  611.1 3.8 bitcast_add_fusion.8
  625.0 3.8 bitcast_add_fusion.8
  628.8 6.5 multiply_convert_fusion.1
  645.1 9.4 gather_fusion.5
  654.5 9.2 gather_fusion.9
  665.3 9.2 gather_fusion.7
  678.0 9.1 gather_fusion.11
  687.2 18.4 %fusion.105 = f32[224,128,128]{2,1,0:T(8,128)} fusion(bf16[224,256,128]{2,1,0:T(8,128)(2,1)} %gather_fusion.7, pred[224]{0:T(512)(128)(4,1)S(1)} %get-tuple-element.961, bf16[224,256,128]{2,1,0:T(8,128)(2,1)} %gather_fusion.5, pred[224]{0:T(512)(128)(4,1)S(1)} %get-tuple-element.963, f32[224]{0:T(256)S(1)} %get-tuple-element.960), kind=kOutput, calls=%fused_computation.141 | convolution fusion | flops 1897398272 | bytes 44041536 | tf_op jit(solution)/shard_map/tsk,tsn->skn/dot_general | solution.py:144
  705.6 18.5 %fusion.110 = f32[224,128,128]{2,1,0:T(8,128)} fusion(bf16[224,256,128]{2,1,0:T(8,128)(2,1)} %gather_fusion.11, pred[224]{0:T(512)(128)(4,1)S(1)} %get-tuple-element.944, bf16[224,256,128]{2,1,0:T(8,128)(2,1)} %gather_fusion.9, pred[224]{0:T(512)(128)(4,1)S(1)} %get-tuple-element.941, f32[224]{0:T(256)S(1)} %get-tuple-element.959), kind=kOutput, calls=%fused_computation.142 | convolution fusion | flops 1897398272 | bytes 44041536 | tf_op jit(solution)/shard_map/tsk,tsn->skn/dot_general | solution.py:144
  724.1 10.1 fusion.115
  734.2 192.1 %while.62 = (s32[]{:T(128)}, f32[128,32,128]{2,1,0:T(8,128)}, s32[448]{0:T(512)S(1)}, s32[]{:T(128)}, bf16[448,128,128]{2,1,0:T(8,128)(2,1)}, /*index=5*/s32[448...) while((s32[]{:T(128)}, f32[128,32,128]{2,1,0:T(8,128)}, ...), condition=%wide.region_5.8_spmd.clone.clone, body=%wide.region_4.0_spmd.clone.clone.sunk | while | flops 205526272 | bytes 20976992 | solution.py:66
  757.1 3.9 bitcast_add_fusion.10
  770.9 3.9 bitcast_add_fusion.10
  784.7 3.9 bitcast_add_fusion.10
  798.5 3.9 bitcast_add_fusion.10
  812.2 3.9 bitcast_add_fusion.10
  826.0 3.9 bitcast_add_fusion.10
  839.8 3.9 bitcast_add_fusion.10
  853.5 3.9 bitcast_add_fusion.10
  867.3 3.9 bitcast_add_fusion.10
  881.1 3.9 bitcast_add_fusion.10
  894.8 3.9 bitcast_add_fusion.10
  908.6 3.9 bitcast_add_fusion.10
  922.4 3.9 bitcast_add_fusion.10
  926.2 8.6 fusion.90
  934.9 5.1 copy-done.7
  945.5 186.0 %while.63 = (s32[]{:T(128)}, f32[128,32,128]{2,1,0:T(8,128)}, s32[448]{0:T(512)}, s32[]{:T(128)}, bf16[448,128,128]{2,1,0:T(8,128)(2,1)}, /*index=5*/s32[448]{0:...) while((s32[]{:T(128)}, f32[128,32,128]{2,1,0:T(8,128)}, ...), condition=%wide.region_7.10_spmd.clone.clone, body=%wide.region_6.9_spmd.clone.clone.sunk | while | flops 205526272 | bytes 24647044 | solution.py:66
  967.5 3.9 bitcast_add_fusion.11
  980.9 3.9 bitcast_add_fusion.11
  994.2 3.9 bitcast_add_fusion.11
  1007.5 3.9 bitcast_add_fusion.11
  1020.9 3.9 bitcast_add_fusion.11
  1034.2 3.9 bitcast_add_fusion.11
  1047.5 3.9 bitcast_add_fusion.11
  1060.8 3.9 bitcast_add_fusion.11
  1074.2 3.9 bitcast_add_fusion.11
  1087.5 3.9 bitcast_add_fusion.11
  1100.8 3.9 bitcast_add_fusion.11
  1114.2 3.9 bitcast_add_fusion.11
  1127.5 3.9 bitcast_add_fusion.11
  1137.6 5.8 add_bitcast_fusion
  1146.2 12.6 %reduce-scatter.2.cloned.1.call-done = bf16[128,1024]{1,0:T(8,128)(2,1)} async-done(((bf16[128,4096]{1,0:T(8,128)(2,1)}), bf16[128,1024]{1,0:T(8,128)(2,1)}) %reduce-scatter.2.cloned.1.call-update) | async-done | bytes 262160 | tf_op jit(solution)/shard_map/reduce_scatter | solution.py:118
  (553 shorter events, 628.1 us)
Async XLA Ops:
  7.2 22.4 %all-gather.6.cloned.1.call-start = ((), (), s32[]{:S(2)}) async-start(), calls=%async_computation.2 | async-start | bytes 1310720 | tf_op jit(solution)/shard_map/all_gather | solution.py:81
  9.0 1.6 copy-start.9
  9.0 224.4 %all-gather.8.cloned.1.call-start = ((), (), s32[]{:S(2)}) async-start(), calls=%async_computation.3 | async-start | bytes 16515072 | tf_op jit(solution)/shard_map/all_gather | solution.py:87
  9.8 425.8 %all-gather.4.cloned.1.call-start = ((), (), s32[]{:S(2)}) async-start(), calls=%async_computation.1 | async-start | bytes 16515072 | tf_op jit(solution)/shard_map/all_gather | solution.py:86
  10.5 1148.3 %reduce-scatter.2.cloned.1.call-start = ((), (), s32[]{:S(2)}) async-start(), calls=%async_computation.4 | async-start | bytes 1310720 | tf_op jit(solution)/shard_map/reduce_scatter | solution.py:118
  10.6 3.7 copy-start.3
  12.8 220.6 %copy-start.2 = (s32[1,448]{1,0:T(1,128)S(1)}, s32[1,448]{1,0:T(1,128)}, u32[]{:S(2)}) copy-start(s32[1,448]{1,0:T(1,128)} %param.36) | copy-start | bytes 5380
  31.8 611.6 %collective-permute-start = (bf16[128,32,128]{2,0,1:T(8,128)(2,1)}, bf16[128,32,128]{2,0,1:T(8,128)(2,1)}, u32[]{:S(2)}, u32[]{:S(2)}) collective-permute-start(bf16[128,32,128]{2,0,1:T(8,128)(2,1)} %copy.98), channel_id=1, source_target_pairs={{0,4},{4,0},{8,12},{12,8},{16,20},{20,16},{24,28},{28,24},{1,5},{5... | collective-permute-start | bytes 3145736 | tf_op jit(solution)/shard_map/ppermute | solution.py:11
  233.5 202.1 %copy-start = (s32[1,448]{1,0:T(1,128)S(1)}, s32[1,448]{1,0:T(1,128)}, u32[]{:S(2)}) copy-start(s32[1,448]{1,0:T(1,128)} %param.33) | copy-start | bytes 5380
  233.5 202.1 %copy-start.1 = (s32[1,448]{1,0:T(1,128)S(1)}, s32[1,448]{1,0:T(1,128)}, u32[]{:S(2)}) copy-start(s32[1,448]{1,0:T(1,128)} %param.32) | copy-start | bytes 5380
  635.3 41.4 %copy-start.4 = (bf16[128,28,128]{2,0,1:T(8,128)(2,1)}, bf16[128,28,128]{2,0,1:T(8,128)(2,1)S(1)}, u32[]{:S(2)}) copy-start(bf16[128,28,128]{2,0,1:T(8,128)(2,1)S(1)} %get-tuple-element.1284) | copy-start | bytes 2752516
  635.3 28.4 %collective-permute-start.1 = (bf16[128,28,128]{2,0,1:T(8,128)(2,1)}, bf16[128,28,128]{2,0,1:T(8,128)(2,1)}, u32[]{:S(2)}, u32[]{:S(2)}) collective-permute-start(bf16[128,28,128]{2,0,1:T(8,128)(2,1)} %get-tuple-element.1251), channel_id=1, source_target_pairs={{0,4},{4,0},{8,12},{12,8},{16,20},{20,16},{24,28},{28,24},{1,5},{5... | collective-permute-start | bytes 2752520 | tf_op jit(solution)/shard_map/ppermute | solution.py:11
  635.9 40.8 %collective-permute-start.2 = (bf16[128,28,128]{2,0,1:T(8,128)(2,1)S(1)}, bf16[128,28,128]{2,0,1:T(8,128)(2,1)}, u32[]{:S(2)}, u32[]{:S(2)}) collective-permute-start(bf16[128,28,128]{2,0,1:T(8,128)(2,1)S(1)} %get-tuple-element.1284), channel_id=1, source_target_pairs={{0,4},{4,0},{8,12},{12,8},{16,20},{20,16},{24,28},{28,24},{1,5},{5... | collective-permute-start | bytes 2752520 | tf_op jit(solution)/shard_map/ppermute | solution.py:11
  734.2 192.1 %collective-permute-start.3 = (bf16[2,56,2,128,128]{4,3,1,2,0:T(8,128)(2,1)}, bf16[2,56,2,128,128]{4,3,1,2,0:T(8,128)(2,1)}, u32[]{:S(2)}, u32[]{:S(2)}) collective-permute-start(bf16[2,56,2,128,128]{4,3,1,2,0:T(8,128)(2,1)} %fusion.115), channel_id=1, source_target_pairs={{0,8},{4,12},{8,0},{12,4},{16,24},{20,28},{24,16},{28,20},{1,9},{5... | collective-permute-start | bytes 22020104 | tf_op jit(solution)/shard_map/ppermute | solution.py:11
  934.9 5.1 copy-start.7
  940.0 5.5 copy-start.5
  942.7 194.9 %collective-permute-start.4 = (bf16[1,56,2,128,128]{4,3,1,2,0:T(8,128)(2,1)}, bf16[1,56,2,128,128]{4,3,1,2,0:T(8,128)(2,1)}, u32[]{:S(2)}, u32[]{:S(2)}) collective-permute-start(bf16[1,56,2,128,128]{4,3,1,2,0:T(8,128)(2,1)} %dynamic-slice_convert_fusion), channel_id=1, source_target_pairs={{0,16},{4,20},{8,24},{12,28},{16,0},{20,4},{24,8},{28,12},{1,17},{... | collective-permute-start | bytes 11010056 | tf_op jit(solution)/shard_map/ppermute | solution.py:11
  954.9 3.3 copy-start.6
  967.5 3.9 copy-start.6
  980.9 3.9 copy-start.6
  994.2 3.9 copy-start.6
  1007.5 3.9 copy-start.6
  1020.9 3.9 copy-start.6
  1034.2 3.9 copy-start.6
  1047.5 3.9 copy-start.6
  1060.8 3.9 copy-start.6
  1074.2 3.9 copy-start.6
  1087.5 3.9 copy-start.6
  1100.8 3.9 copy-start.6
  1114.2 3.9 copy-start.6
  1127.5 3.9 copy-start.6
  1134.1 1.5 copy-start.8
Sparse Core Ops, SparseCore 0:
  10.1 19.4 all-gather.5
  31.8 201.6 all-gather.7
  235.7 199.8 all-gather.3
  1135.7 23.0 reduce-scatter.1
where the time goes:
time: 1170 us
  matrix products  462 us (39%)
  local copies, waits for them, and re-layouts  359 us (31%)
  waiting for transfers between devices  239 us (20%)
  other arithmetic  82.2 us (7%)
  between operations  15.4 us (1%)
    dot_general x56, matrix products, place_split(): jnp.einsum(form, rest_part, table, preferred_element_type=jnp.float32)  213 us
    all_gather x1, waiting for transfers between devices, on_device(): up_all = lax.all_gather(up_blocks, 'seq', axis=1, tiled=True)  200 us
    convert_element_type x56, local copies, waits for them, and re-layouts, place_split(): rest_part = (products - high_part.astype(jnp.float32)).astype(jnp.bfloat16)  95.1 us
    convert_element_type x56, local copies, waits for them, and re-layouts, place_split(): high_part = products.astype(jnp.bfloat16)  95 us
    dot_general x56, matrix products, place_split(): jnp.einsum(form, high_part, table, preferred_element_type=jnp.float32)  91.5 us
    dot_general x28, matrix products, return_one_group(): jnp.einsum('tsn,skn->tsk', picked, chosen, preferred_element_type=jnp.flo...  60.6 us
    dot_general x28, matrix products, project_one_group(): jnp.einsum('tsk,skn->tsn', picked, chosen, preferred_element_type=jnp.flo...  59.6 us
    gather x28, local copies, waits for them, and re-layouts, project_one_group(): picked = jnp.take(tiles, row_ids, axis=1)  55.3 us
  transfers between devices with their start and end apart: 9, of which 5 were waited for; matrix products, arithmetic and copies ran while one was open for 71% of the time, Pallas kernels for 0%

commit v1 on v0

--- a/solution.py
+++ b/solution.py
@@ -3,6 +3,18 @@
 import jax.numpy as jnp
 from jax import lax
 from jax.sharding import PartitionSpec as P
+
+
+def collect(x, axis, dim):
+    ways, here = (lax.axis_size(axis), lax.axis_index(axis))
+    grown, reach = (x, 1)
+    while reach < ways:
+        theirs = lax.ppermute(grown, axis, [(d, d ^ reach) for d in range(ways)])
+        mine_first = jnp.concatenate([grown, theirs], axis=dim)
+        theirs_first = jnp.concatenate([theirs, grown], axis=dim)
+        grown = jnp.where(here & reach == 0, mine_first, theirs_first)
+        reach = 2 * reach
+    return grown
 
 
 def swapped(value, axis, stride):
@@ -84,7 +96,7 @@
     row_blocks = gathered.shape[1] // block_size
     col_blocks = hidden_grad.shape[1] // block_size
     gate_all = lax.all_gather(gate_blocks, "seq", axis=1, tiled=True)
-    up_all = lax.all_gather(up_blocks, "seq", axis=1, tiled=True)
+    up_all = collect(up_blocks, "seq", 1)
     capacity = gate_all.shape[1]
     group_size = 32
     groups = capacity // group_size

time: 1170 us -> 1590 us (1.36)
  waiting for transfers between devices: 239 us -> 606 us
  other arithmetic: 82.2 us -> 117 us
    ppermute x0 -> x3, waiting for transfers between devices: none -> 591 us  [collect(): theirs = lax.ppermute(grown, axis, [(d, d ^ reach) for d in range(ways)])]
    all_gather x1 -> x0, waiting for transfers between devices: 200 us -> none  [on_device(): up_all = lax.all_gather(up_blocks, 'seq', axis=1, tiled=True)]
    select_n x0 -> x5, other arithmetic: none -> 34.4 us  [collect(): grown = jnp.where(here & reach == 0, mine_first, theirs_first)]
  transfers between devices with their start and end apart: 9 -> 11, of which waited for: 5 -> 5; matrix products, arithmetic and copies ran while one was open for 71% -> 54% of each run, Pallas kernels for 0% -> 0%
where the time goes in v1:
time: 1590 us; the launch traced here: 1570 us
  waiting for transfers between devices  606 us (38%)
  matrix products  460 us (29%)
  local copies, waits for them, and re-layouts  356 us (22%)
  other arithmetic  117 us (7%)
    ppermute x3, waiting for transfers between devices, collect(): theirs = lax.ppermute(grown, axis, [(d, d ^ reach) for d in range(ways)])  591 us
    dot_general x56, matrix products, place_split(): jnp.einsum(form, rest_part, table, preferred_element_type=jnp.float32)  211 us
    convert_element_type x56, local copies, waits for them, and re-layouts, place_split(): rest_part = (products - high_part.astype(jnp.float32)).astype(jnp.bfloat16)  94.2 us
    convert_element_type x56, local copies, waits for them, and re-layouts, place_split(): high_part = products.astype(jnp.bfloat16)  94.2 us
    dot_general x56, matrix products, place_split(): jnp.einsum(form, high_part, table, preferred_element_type=jnp.float32)  91.4 us
    dot_general x28, matrix products, return_one_group(): jnp.einsum('tsn,skn->tsk', picked, chosen, preferred_element_type=jnp.flo...  60.7 us
    dot_general x28, matrix products, project_one_group(): jnp.einsum('tsk,skn->tsn', picked, chosen, preferred_element_type=jnp.flo...  59.5 us
    gather x28, local copies, waits for them, and re-layouts, project_one_group(): picked = jnp.take(tiles, row_ids, axis=1)  55.3 us
  transfers between devices with their start and end apart: 11, of which 5 were waited for; matrix products, arithmetic and copies ran while one was open for 54% of the time, Pallas kernels for 0%

profile of v1, /device:TPU:0, one launch (start us, length us, event | category | flops | bytes accessed | tf_op | source)
XLA Modules:
  0.0 1572.4 jit_solution(13205571290445734023)
XLA Ops:
  10.2 40.3 %collective-permute-done = bf16[1,56,128,128]{3,2,1,0:T(8,128)(2,1)} collective-permute-done((bf16[1,56,128,128]{3,2,1,0:T(8,128)(2,1)}, bf16[1,56,128,128]{3,2,1,0:T(8,128)(2,1)}, u32[]{:S(2)}, u32[]{:S(2)}) %collective-permute-start) | collective-permute-done | bytes 1835040 | tf_op jit(solution)/shard_map/ppermute | solution.py:12
  50.6 4.8 maximum_select_fusion.4
  60.5 75.6 %collective-permute-done.1 = bf16[1,112,128,128]{3,2,1,0:T(8,128)(2,1)} collective-permute-done((bf16[1,112,128,128]{3,2,1,0:T(8,128)(2,1)}, bf16[1,112,128,128]{3,2,1,0:T(8,128)(2,1)}, u32[]{:S(2)}, u32[]{:S(2)}) %collective-permute-start.1) | collective-permute-done | bytes 3670048 | tf_op jit(solution)/shard_map/ppermute | solution.py:12
  136.2 7.0 maximum_select_fusion.2
  155.4 6.5 maximum_select_fusion.1
  161.9 475.5 %collective-permute-done.2 = bf16[1,224,128,128]{3,2,1,0:T(8,128)(2,1)} collective-permute-done((bf16[1,224,128,128]{3,2,1,0:T(8,128)(2,1)}, bf16[1,224,128,128]{3,2,1,0:T(8,128)(2,1)}, u32[]{:S(2)}, u32[]{:S(2)}) %collective-permute-start.2) | collective-permute-done | bytes 7340064 | tf_op jit(solution)/shard_map/ppermute | solution.py:12
  637.4 13.7 maximum_select_fusion
  651.1 189.2 %while.61 = (s32[]{:T(128)}, f32[128,28,128]{2,1,0:T(8,128)}, s32[448]{0:T(512)S(1)}, s32[]{:T(128)}, bf16[448,128,128]{2,1,0:T(8,128)(2,1)}, /*index=5*/s32[448...) while((s32[]{:T(128)}, f32[128,28,128]{2,1,0:T(8,128)}, ...), condition=%wide.region_3.5_spmd.clone, body=%wide.region_2.4_spmd.clone.sunk | while | flops 196940544 | bytes 19928416 | solution.py:57
  674.0 3.6 bitcast_add_fusion.9
  701.1 3.6 bitcast_add_fusion.9
  840.3 192.6 %while.60 = (s32[]{:T(128)}, f32[128,28,128]{2,1,0:T(8,128)}, s32[448]{0:T(512)S(1)}, s32[]{:T(128)}, bf16[448,128,128]{2,1,0:T(8,128)(2,1)}, /*index=5*/s32[448...) while((s32[]{:T(128)}, f32[128,28,128]{2,1,0:T(8,128)}, ...), condition=%wide.region_1.3_spmd.clone, body=%wide.region_0.2_spmd.clone.sunk | while | flops 196940544 | bytes 19928416 | solution.py:57
  863.4 3.8 bitcast_add_fusion.8
  877.2 3.8 bitcast_add_fusion.8
  891.0 3.8 bitcast_add_fusion.8
  904.8 3.8 bitcast_add_fusion.8
  918.6 3.8 bitcast_add_fusion.8
  932.4 3.8 bitcast_add_fusion.8
  946.2 3.8 bitcast_add_fusion.8
  960.0 3.8 bitcast_add_fusion.8
  973.8 3.8 bitcast_add_fusion.8
  987.6 3.8 bitcast_add_fusion.8
  1001.4 3.8 bitcast_add_fusion.8
  1015.2 3.8 bitcast_add_fusion.8
  1029.0 3.8 bitcast_add_fusion.8
  1032.9 6.5 multiply_convert_fusion.1
  1049.1 9.4 gather_fusion.5
  1058.5 9.2 gather_fusion.9
  1069.3 9.2 gather_fusion.7
  1082.3 9.1 gather_fusion.11
  1091.4 18.4 %fusion.105 = f32[224,128,128]{2,1,0:T(8,128)} fusion(bf16[224,256,128]{2,1,0:T(8,128)(2,1)} %gather_fusion.7, pred[224]{0:T(512)(128)(4,1)S(1)} %get-tuple-element.961, bf16[224,256,128]{2,1,0:T(8,128)(2,1)} %gather_fusion.5, pred[224]{0:T(512)(128)(4,1)S(1)} %get-tuple-element.963, f32[224]{0:T(256)S(1)} %get-tuple-element.960), kind=kOutput, calls=%fused_computation.142 | convolution fusion | flops 1897398272 | bytes 44041536 | tf_op jit(solution)/shard_map/tsk,tsn->skn/dot_general | solution.py:156
  1109.9 18.6 %fusion.110 = f32[224,128,128]{2,1,0:T(8,128)} fusion(bf16[224,256,128]{2,1,0:T(8,128)(2,1)} %gather_fusion.11, pred[224]{0:T(512)(128)(4,1)S(1)} %get-tuple-element.944, bf16[224,256,128]{2,1,0:T(8,128)(2,1)} %gather_fusion.9, pred[224]{0:T(512)(128)(4,1)S(1)} %get-tuple-element.941, f32[224]{0:T(256)S(1)} %get-tuple-element.959), kind=kOutput, calls=%fused_computation.143 | convolution fusion | flops 1897398272 | bytes 44041536 | tf_op jit(solution)/shard_map/tsk,tsn->skn/dot_general | solution.py:156
  1128.5 10.1 fusion.115
  1139.6 192.4 %while.62 = (s32[]{:T(128)}, f32[128,32,128]{2,1,0:T(8,128)}, s32[448]{0:T(512)S(1)}, s32[]{:T(128)}, bf16[448,128,128]{2,1,0:T(8,128)(2,1)}, /*index=5*/s32[448...) while((s32[]{:T(128)}, f32[128,32,128]{2,1,0:T(8,128)}, ...), condition=%wide.region_5.8_spmd.clone.clone, body=%wide.region_4.7_spmd.clone.clone.sunk | while | flops 205526272 | bytes 20976992 | solution.py:78
  1162.6 3.9 bitcast_add_fusion.10
  1176.4 3.9 bitcast_add_fusion.10
  1190.2 3.9 bitcast_add_fusion.10
  1204.0 3.9 bitcast_add_fusion.10
  1217.8 3.9 bitcast_add_fusion.10
  1231.6 3.9 bitcast_add_fusion.10
  1245.4 3.9 bitcast_add_fusion.10
  1259.2 3.9 bitcast_add_fusion.10
  1273.0 3.9 bitcast_add_fusion.10
  1286.8 3.9 bitcast_add_fusion.10
  1300.6 3.9 bitcast_add_fusion.10
  1314.4 3.9 bitcast_add_fusion.10
  1328.2 3.9 bitcast_add_fusion.10
  1332.1 8.6 fusion.90
  1340.7 5.1 copy-done.7
  1351.9 186.2 %while.63 = (s32[]{:T(128)}, f32[128,32,128]{2,1,0:T(8,128)}, s32[448]{0:T(512)}, s32[]{:T(128)}, bf16[448,128,128]{2,1,0:T(8,128)(2,1)}, /*index=5*/s32[448]{0:...) while((s32[]{:T(128)}, f32[128,32,128]{2,1,0:T(8,128)}, ...), condition=%wide.region_7.10_spmd.clone.clone, body=%wide.region_6.9_spmd.clone.clone.sunk | while | flops 205526272 | bytes 24647044 | solution.py:78
  1374.0 3.9 bitcast_add_fusion.11
  1387.4 3.9 bitcast_add_fusion.11
  1400.7 3.9 bitcast_add_fusion.11
  1414.0 3.9 bitcast_add_fusion.11
  1427.4 3.9 bitcast_add_fusion.11
  1440.7 3.9 bitcast_add_fusion.11
  1454.1 3.9 bitcast_add_fusion.11
  1467.4 3.9 bitcast_add_fusion.11
  1480.8 3.9 bitcast_add_fusion.11
  1494.1 3.9 bitcast_add_fusion.11
  1507.5 3.9 bitcast_add_fusion.11
  1520.8 3.9 bitcast_add_fusion.11
  1534.2 3.9 bitcast_add_fusion.11
  1544.3 5.8 add_bitcast_fusion
  1553.0 12.5 reduce-scatter.2.cloned.1.call-done
  (567 shorter events, 649.9 us)
Async XLA Ops:
  7.2 144.3 %all-gather.5.cloned.1.call-start = ((), (), s32[]{:S(2)}) async-start(), calls=%async_computation.2 | async-start | bytes 1310720 | tf_op jit(solution)/shard_map/all_gather | solution.py:93
  7.2 43.4 %collective-permute-start = (bf16[1,56,128,128]{3,2,1,0:T(8,128)(2,1)}, bf16[1,56,128,128]{3,2,1,0:T(8,128)(2,1)}, u32[]{:S(2)}, u32[]{:S(2)}) collective-permute-start(bf16[1,56,128,128]{3,2,1,0:T(8,128)(2,1)} %param.31), channel_id=1, source_target_pairs={{0,4},{4,0},{8,12},{12,8},{16,20},{20,16},{24,28},{28,24},{1,5},{5... | collective-permute-start | bytes 5505032 | tf_op jit(solution)/shard_map/ppermute | solution.py:12
  10.2 46.9 %copy-start.12 = (bf16[128,1024]{1,0:T(8,128)(2,1)S(1)}, bf16[128,1024]{1,0:T(8,128)(2,1)}, u32[]{:S(2)}) copy-start(bf16[128,1024]{1,0:T(8,128)(2,1)} %param.28) | copy-start | bytes 786436
  10.2 47.8 %copy-start.9 = (bf16[1,56,128,128]{3,2,1,0:T(8,128)(2,1)S(1)}, bf16[1,56,128,128]{3,2,1,0:T(8,128)(2,1)}, u32[]{:S(2)}) copy-start(bf16[1,56,128,128]{3,2,1,0:T(8,128)(2,1)} %param.31) | copy-start | bytes 5505028
  55.3 80.8 %collective-permute-start.1 = (bf16[1,112,128,128]{3,2,1,0:T(8,128)(2,1)}, bf16[1,112,128,128]{3,2,1,0:T(8,128)(2,1)}, u32[]{:S(2)}, u32[]{:S(2)}) collective-permute-start(bf16[1,112,128,128]{3,2,1,0:T(8,128)(2,1)} %maximum_select_fusion.4), channel_id=1, source_target_pairs={{0,8},{4,12},{8,0},{12,4},{16,24},{20,28},{24,16},{28,20},{1,9},{5... | collective-permute-start | bytes 11010056 | tf_op jit(solution)/shard_map/ppermute | solution.py:12
  58.0 782.3 %all-gather.3.cloned.1.call-start = ((), (), s32[]{:S(2)}) async-start(), calls=%async_computation.1 | async-start | bytes 16515072 | tf_op jit(solution)/shard_map/all_gather | solution.py:98
  60.5 82.6 %copy-start.8 = (bf16[112,128,128]{2,1,0:T(8,128)(2,1)}, bf16[112,128,128]{2,1,0:T(8,128)(2,1)S(1)}, u32[]{:S(2)}) copy-start(bf16[112,128,128]{2,1,0:T(8,128)(2,1)S(1)} %maximum_select_fusion.3) | copy-start | bytes 11010052
  136.2 9.7 copy-start.11
  143.1 6.4 copy-start.3
  143.1 494.3 %collective-permute-start.2 = (bf16[1,224,128,128]{3,2,1,0:T(8,128)(2,1)}, bf16[1,224,128,128]{3,2,1,0:T(8,128)(2,1)}, u32[]{:S(2)}, u32[]{:S(2)}) collective-permute-start(bf16[1,224,128,128]{3,2,1,0:T(8,128)(2,1)} %maximum_select_fusion.2), channel_id=1, source_target_pairs={{0,16},{4,20},{8,24},{12,28},{16,0},{20,4},{24,8},{28,12},{1,17},{... | collective-permute-start | bytes 22020104 | tf_op jit(solution)/shard_map/ppermute | solution.py:12
  145.7 1419.8 %reduce-scatter.2.cloned.1.call-start = ((), (), s32[]{:S(2)}) async-start(), calls=%async_computation.3 | async-start | bytes 1310720 | tf_op jit(solution)/shard_map/reduce_scatter | solution.py:130
  153.9 893.6 %collective-permute-start.3 = (bf16[128,32,128]{2,0,1:T(8,128)(2,1)}, bf16[128,32,128]{2,0,1:T(8,128)(2,1)}, u32[]{:S(2)}, u32[]{:S(2)}) collective-permute-start(bf16[128,32,128]{2,0,1:T(8,128)(2,1)} %copy.98), channel_id=1, source_target_pairs={{0,4},{4,0},{8,12},{12,8},{16,20},{20,16},{24,28},{28,24},{1,5},{5... | collective-permute-start | bytes 3145736 | tf_op jit(solution)/shard_map/ppermute | solution.py:23
  637.4 13.7 copy-start.2
  651.1 189.2 %copy-start = (s32[1,448]{1,0:T(1,128)S(1)}, s32[1,448]{1,0:T(1,128)}, u32[]{:S(2)}) copy-start(s32[1,448]{1,0:T(1,128)} %param.33) | copy-start | bytes 5380
  651.1 189.2 %copy-start.1 = (s32[1,448]{1,0:T(1,128)S(1)}, s32[1,448]{1,0:T(1,128)}, u32[]{:S(2)}) copy-start(s32[1,448]{1,0:T(1,128)} %param.32) | copy-start | bytes 5380
  1039.4 41.6 %copy-start.4 = (bf16[128,28,128]{2,0,1:T(8,128)(2,1)}, bf16[128,28,128]{2,0,1:T(8,128)(2,1)S(1)}, u32[]{:S(2)}) copy-start(bf16[128,28,128]{2,0,1:T(8,128)(2,1)S(1)} %get-tuple-element.1284) | copy-start | bytes 2752516
  1039.4 28.4 %collective-permute-start.4 = (bf16[128,28,128]{2,0,1:T(8,128)(2,1)}, bf16[128,28,128]{2,0,1:T(8,128)(2,1)}, u32[]{:S(2)}, u32[]{:S(2)}) collective-permute-start(bf16[128,28,128]{2,0,1:T(8,128)(2,1)} %get-tuple-element.1251), channel_id=1, source_target_pairs={{0,4},{4,0},{8,12},{12,8},{16,20},{20,16},{24,28},{28,24},{1,5},{5... | collective-permute-start | bytes 2752520 | tf_op jit(solution)/shard_map/ppermute | solution.py:23
  1040.6 40.4 %collective-permute-start.5 = (bf16[128,28,128]{2,0,1:T(8,128)(2,1)S(1)}, bf16[128,28,128]{2,0,1:T(8,128)(2,1)}, u32[]{:S(2)}, u32[]{:S(2)}) collective-permute-start(bf16[128,28,128]{2,0,1:T(8,128)(2,1)S(1)} %get-tuple-element.1284), channel_id=1, source_target_pairs={{0,4},{4,0},{8,12},{12,8},{16,20},{20,16},{24,28},{28,24},{1,5},{5... | collective-permute-start | bytes 2752520 | tf_op jit(solution)/shard_map/ppermute | solution.py:23
  1138.6 193.5 %collective-permute-start.6 = (bf16[2,56,2,128,128]{4,3,1,2,0:T(8,128)(2,1)}, bf16[2,56,2,128,128]{4,3,1,2,0:T(8,128)(2,1)}, u32[]{:S(2)}, u32[]{:S(2)}) collective-permute-start(bf16[2,56,2,128,128]{4,3,1,2,0:T(8,128)(2,1)} %fusion.115), channel_id=1, source_target_pairs={{0,8},{4,12},{8,0},{12,4},{16,24},{20,28},{24,16},{28,20},{1,9},{5... | collective-permute-start | bytes 22020104 | tf_op jit(solution)/shard_map/ppermute | solution.py:23
  1340.7 5.2 copy-start.7
  1345.8 6.1 copy-start.5
  1348.6 195.8 %collective-permute-start.7 = (bf16[1,56,2,128,128]{4,3,1,2,0:T(8,128)(2,1)}, bf16[1,56,2,128,128]{4,3,1,2,0:T(8,128)(2,1)}, u32[]{:S(2)}, u32[]{:S(2)}) collective-permute-start(bf16[1,56,2,128,128]{4,3,1,2,0:T(8,128)(2,1)} %dynamic-slice_convert_fusion), channel_id=1, source_target_pairs={{0,16},{4,20},{8,24},{12,28},{16,0},{20,4},{24,8},{28,12},{1,17},{... | collective-permute-start | bytes 11010056 | tf_op jit(solution)/shard_map/ppermute | solution.py:23
  1361.3 3.3 copy-start.6
  1374.0 3.9 copy-start.6
  1387.4 3.9 copy-start.6
  1400.7 3.9 copy-start.6
  1414.0 3.9 copy-start.6
  1427.4 3.9 copy-start.6
  1440.7 3.9 copy-start.6
  1454.1 3.9 copy-start.6
  1467.4 3.9 copy-start.6
  1480.8 3.9 copy-start.6
  1494.1 3.9 copy-start.6
  1507.5 3.9 copy-start.6
  1520.8 3.9 copy-start.6
  1534.2 3.9 copy-start.6
  1538.1 4.3 copy-start.10
Sparse Core Ops, SparseCore 0:
  58.2 16.9 all-gather.4
  145.8 432.7 all-gather.2
  1542.5 22.9 reduce-scatter.1
